TPU v7x, 512 devices: a whole 4x4x16 slice. The times are simulated.
512 devices in a mesh: rows: 128 (over x, z, core), rhs: 4 (over y).
Axes of the slice: x: 4, y: 4, z: 16, core: 2. Of those that a mesh axis runs over, the one named last changes fastest.
Arguments:
- targets: float32 [32768, 1024], P(('rows', 'rhs')), may hold values from -6 to 6
- send_order: int32 [32768], P('rows'), may hold values from 0 to 255, as said below
- send_count: int32 [128, 128], P('rows'), may hold values from 0 to 4, as said below
- recv_slot: int32 [32768], P('rows'), may hold values from 0 to 255, as said below
- panel: float32 [32768, 4096], P('rows'), may hold values from -0.09375 to 0.09375
- inv_diag: float32 [4, 1024, 1024], P(None, None, 'rows'), may hold values from -0.075 to 1.4, as said below
Outputs:
- solution: float32 [32768, 1024], P('rows', 'rhs')
Inputs may be any that keep to these rules, and one draw needn't show every extreme that they name: For each rows index a, send_order[a * 256 : (a + 1) * 256] is a permutation of 0 .. 255 whose destinations (as the steps define them) do not fall. Each row and each column of send_count sums to 256; some entry equals 4. There are a permutation p of the rows indices and a table h with send_count[a, p(j)] = h[(j - a) mod 128]. `recv_slot`: every rows index receives each slot 0 .. 255 exactly once. Each inv_diag[k] is lower triangular with diagonal entries from 0.6 to 1.4 and entries below the diagonal within -0.075 to 0.075.
All inputs are finite; a program needn't handle non-finite values.
Results may differ from a plain program's by a relative error of at most 0.0001.
Values sent between devices are 32-bit elements; how exact they have to be, the bound alone decides.
No kernel may reach another device: no remote copies, remote signals or barrier semaphores. Data moves between devices by JAX's collectives and lax.ppermute only.
A program may use at most 64 MiB of HBM per device.

v0:
```python
import jax
import jax.numpy as jnp
from jax import lax
from jax.sharding import Mesh, PartitionSpec as P

ROWS = ("x", "z", "core")
SWAP = [(0, 1), (1, 0)]


def product(left, right, contract=((1,), (0,))):
    return lax.dot_general(
        left,
        right,
        (contract, ((), ())),
        precision=lax.Precision.HIGHEST,
        preferred_element_type=jnp.float32,
    )


def redistribute(targets, send_order, send_count, recv_slot):
    groups = lax.axis_size(ROWS)
    arrived = lax.all_to_all(targets, "rhs", split_axis=1, concat_axis=0, tiled=True)
    rows_local, columns = arrived.shape
    capacity, tag = (4, 64)
    counts = send_count[0]
    dest = jnp.arange(groups, dtype=jnp.int32)
    starts = jnp.sum(jnp.where(dest[None, :] < dest[:, None], counts[None, :], 0), axis=1)
    index = jnp.arange(rows_local, dtype=jnp.int32)
    position = jnp.sum(jnp.where(send_order[:, None] == index[None, :], index[:, None], 0), axis=0)
    slot_number = jnp.arange(capacity, dtype=jnp.int32)
    listed = starts[None, :] + slot_number[:, None]
    listed = jnp.where(slot_number[:, None] < counts[None, :], listed, -1)
    picked = (listed[:, :, None] == position[None, None, :]).astype(jnp.float32)
    picked = picked.reshape(capacity * groups, rows_local)
    landing = jnp.broadcast_to((recv_slot + 1).astype(jnp.float32)[:, None], (rows_local, 2 * tag))
    planes = product(picked, jnp.concatenate([arrived, landing], axis=1))
    planes = planes.reshape(capacity, groups, columns + 2 * tag)
    halves = [
        jnp.concatenate(
            [
                planes[s, :, :columns],
                planes[s + 1, :, :columns],
                planes[s, :, columns : columns + tag],
                planes[s + 1, :, columns : columns + tag],
            ],
            axis=1,
        )
        for s in range(0, capacity, 2)
    ]
    incoming = lax.all_to_all(
        jnp.stack(halves, axis=1), ROWS, split_axis=0, concat_axis=0, tiled=True
    )
    total = 0.0
    for h in range(capacity // 2):
        half = incoming[:, h]
        for s in range(2):
            label = half[:, 2 * columns + s * tag : 2 * columns + s * tag + 1] - 1.0
            placed = (label.astype(jnp.int32) == index[None, :]).astype(jnp.float32)
            rows = half[:, s * columns : (s + 1) * columns]
            total = total + product(placed, rows, ((0,), (0,)))
    return total


def shards(targets, send_order, send_count, recv_slot, panel, inv_diag):
    sections, block_rows, share = inv_diag.shape
    nx, nz, nc = (lax.axis_size(a) for a in ROWS)
    zi = lax.axis_index("z")
    first = lax.axis_index("core") == 0
    even = zi % 2 == 0
    square = sections * share
    inverse_columns = jnp.swapaxes(inv_diag, 1, 2)

    def tile(j, k):
        if j == k:
            return inverse_columns[k]
        return panel[j * share : (j + 1) * share, k * block_rows : (k + 1) * block_rows]

    weight = {}
    early = [(0, 0), (1, 0)]
    late = [(j, k) for j in range(sections) for k in range(j + 1) if (j, k) not in early]
    for names in (early, late):
        gathered = lax.all_gather(jnp.stack([tile(j, k) for j, k in names]), "z")
        for i, name in enumerate(names):
            weight[name] = gathered[:, i].reshape(nz * share, block_rows)
    residual = redistribute(targets, send_order, send_count, recv_slot)
    columns = residual.shape[1] // 2
    halves = jnp.stack([residual[:square, :columns], residual[:square, columns:]])
    tops = jnp.broadcast_to(halves[None], (nz // 2,) + halves.shape).reshape(nz, square, columns)
    tops = lax.all_to_all(tops, "z", split_axis=0, concat_axis=0, tiled=True)
    pending = [
        tops[:, k * share : (k + 1) * share].reshape(nz * share, columns) for k in range(sections)
    ]
    left, right = (residual[square:, :columns], residual[square:, columns:])
    below = [jnp.where(even, left, right), jnp.where(even, right, left)]
    start = ((lax.axis_index("x") * nz + zi) * nc + lax.axis_index("core")) * share
    finished = []
    for k in range(sections):
        partial = product(weight[k, k], pending[k], ((0,), (0,)))
        partial = partial.reshape(nx * nz, nc, share, columns)
        keep = jnp.where(first, partial[:, 0], partial[:, 1])
        give = jnp.where(first, partial[:, 1], partial[:, 0])
        half = keep + lax.ppermute(give, "core", SWAP)
        copies = jnp.broadcast_to(half[None], (nx,) + half.shape)
        mine = jnp.sum(lax.all_to_all(copies, "x", split_axis=0, concat_axis=0, tiled=True), axis=0)
        other = lax.ppermute(mine, "core", SWAP)
        solved = jnp.stack([jnp.where(first, mine, other), jnp.where(first, other, mine)], axis=1)
        solved = solved.reshape(block_rows, columns)
        for j in range(k + 1, sections):
            pending[j] = pending[j] - product(weight[j, k], solved)
        traded = lax.ppermute(solved, "z", [(i, i ^ 1) for i in range(nz)])
        factor = panel[square:, k * block_rows : (k + 1) * block_rows]
        pieces = []
        for h, block in enumerate((solved, traded)):
            below[h] = below[h] - product(factor, block)
            pieces.append(lax.dynamic_slice_in_dim(block, start, share, 0))
        finished.append(pieces)
    ends = [jnp.concatenate([f[h] for f in finished] + [below[h]], axis=0) for h in range(2)]
    return jnp.concatenate(
        [jnp.where(even, ends[0], ends[1]), jnp.where(even, ends[1], ends[0])], axis=1
    )


def solution(mesh):
    ny = mesh.shape["rhs"]
    split = Mesh(mesh.devices.reshape(4, 16, 2, ny), ROWS + ("rhs",))
    placed = (
        P(ROWS + ("rhs",), None),
        P(ROWS),
        P(ROWS, None),
        P(ROWS),
        P(ROWS, None),
        P(None, None, ROWS),
    )
    return jax.shard_map(
        shards, mesh=split, in_specs=placed, out_specs=P(ROWS, "rhs"), check_vma=False
    )
```

profile of v0, /device:TPU:1, one launch (start us, length us, event | category | flops | bytes accessed | tf_op | source)
XLA Modules:
  0.0 300.6 jit_solution(726331077672846849)
XLA Ops:
  6.5 0.8 slice_bitcast_fusion.29
  7.3 0.8 constant_dynamic-update-slice_fusion.7
  8.1 0.8 constant_dynamic-update-slice_fusion.6
  8.8 0.8 constant_dynamic-update-slice_fusion.5
  9.6 0.8 constant_dynamic-update-slice_fusion.4
  10.3 0.8 constant_dynamic-update-slice_fusion.3
  11.1 0.8 constant_dynamic-update-slice_fusion.2
  11.9 0.8 constant_dynamic-update-slice_fusion.1
  12.6 0.8 constant_dynamic-update-slice_fusion
  14.1 1.7 copy.128
  15.8 5.0 %all-to-all-start = ((f32[64,4,256]{2,0,1:T(8,128)}), f32[64,4,256]{2,0,1:T(8,128)S(1)}, u32[]{:S(2)}, u32[]{:S(2)}) async-start(f32[64,4,256]{2,0,1:T(8,128)} %bitcast.223), calls=%async_computation | async-start | bytes 524288 | tf_op jit(solution)/shard_map/all_to_all | solution.py:22
  20.8 0.8 select_reduce_fusion.1
  21.6 0.8 select_reduce_fusion
  23.7 2.6 all-to-all-done
  27.3 1.4 copy.87
  28.7 21.0 %all-to-all-start.1 = ((f32[128,2,640]{2,1,0:T(2,128)}), f32[128,2,640]{2,1,0:T(2,128)S(1)}, u32[]{:S(2)}, u32[]{:S(2)}) async-start(f32[128,2,640]{2,1,0:T(2,128)} %copy.87), calls=%async_computation.1 | async-start | bytes 1310720 | tf_op jit(solution)/shard_map/all_to_all | solution.py:50
  50.4 43.7 %all-to-all-done.1 = f32[128,2,640]{2,1,0:T(2,128)S(1)} async-done(((f32[128,2,640]{2,1,0:T(2,128)}), f32[128,2,640]{2,1,0:T(2,128)S(1)}, u32[]{:S(2)}, u32[]{:S(2)}) %all-to-all-start.1) | async-done | bytes 655392 | tf_op jit(solution)/shard_map/all_to_all | solution.py:50
  97.4 4.1 %all-to-all-start.2 = ((f32[16,32,128]{2,1,0:T(8,128)}), f32[16,32,128]{2,1,0:T(8,128)S(1)}, u32[]{:S(2)}, u32[]{:S(2)}) async-start(f32[16,32,128]{2,1,0:T(8,128)} %bitcast.23), calls=%async_computation.2 | async-start | bytes 524288 | tf_op jit(solution)/shard_map/all_to_all | solution.py:89
  101.5 1.1 slice_bitcast_fusion.15
  102.8 12.3 %all-to-all-done.2 = f32[16,32,128]{2,1,0:T(8,128)S(1)} async-done(((f32[16,32,128]{2,1,0:T(8,128)}), f32[16,32,128]{2,1,0:T(8,128)S(1)}, u32[]{:S(2)}, u32[]{:S(2)}) %all-to-all-start.2) | async-done | bytes 262176 | tf_op jit(solution)/shard_map/all_to_all | solution.py:89
  115.7 7.5 %collective-permute-start = (f32[64,8,128]{2,1,0:T(8,128)S(1)}, f32[64,8,128]{2,1,0:T(8,128)S(1)}, u32[]{:S(2)}, u32[]{:S(2)}) collective-permute-start(f32[64,8,128]{2,1,0:T(8,128)S(1)} %select_bitcast_fusion.11), channel_id=1, source_target_pairs={{0,4},{4,0},{1,5},{5,1},{2,6},{6,2},{3,7},{7,3},{8,12},{12,8},{9,1... | collective-permute-start | bytes 786440 | tf_op jit(solution)/shard_map/ppermute | solution.py:102
  123.2 1.1 collective-permute-done
  124.5 17.7 %all_to_all.49 = f32[4,64,8,128]{3,2,1,0:T(8,128)S(1)} all-to-all(f32[4,64,8,128]{3,2,1,0:T(8,128)S(1)} %broadcast_in_dim.47), channel_id=1, replica_groups=mesh['x'=4,'z'=16,'core'=2,'rhs'=4] {'x'}, dimensions={0} | all-to-all | bytes 2097152 | tf_op jit(solution)/shard_map/all_to_all | solution.py:104
  142.2 3.7 %collective-permute-start.1 = (f32[64,8,128]{2,1,0:T(8,128)S(1)}, f32[64,8,128]{2,1,0:T(8,128)S(1)}, u32[]{:S(2)}, u32[]{:S(2)}) collective-permute-start(f32[64,8,128]{2,1,0:T(8,128)S(1)} %reduce_sum.56), channel_id=1, source_target_pairs={{0,4},{4,0},{1,5},{5,1},{2,6},{6,2},{3,7},{7,3},{8,12},{12,8},{9,1... | collective-permute-start | bytes 786440 | tf_op jit(solution)/shard_map/ppermute | solution.py:105
  145.9 1.1 collective-permute-done.1
  147.9 20.6 %all-gather.7.cloned.1.call-done = f32[128,8,1024]{2,1,0:T(8,128)} async-done(((f32[8,8,1024]{2,1,0:T(8,128)}), f32[128,8,1024]{2,1,0:T(8,128)}) %all-gather.7.cloned.1.call-update) | async-done | bytes 4194320 | tf_op jit(solution)/shard_map/all_gather | solution.py:82
  168.5 1.5 slice_bitcast_fusion.6
  170.8 10.6 %collective-permute-start.2 = (f32[64,8,128]{2,1,0:T(8,128)S(1)}, f32[64,8,128]{2,1,0:T(8,128)S(1)}, u32[]{:S(2)}, u32[]{:S(2)}) collective-permute-start(f32[64,8,128]{2,1,0:T(8,128)S(1)} %select_bitcast_fusion.8), channel_id=1, source_target_pairs={{0,4},{4,0},{1,5},{5,1},{2,6},{6,2},{3,7},{7,3},{8,12},{12,8},{9,1... | collective-permute-start | bytes 786440 | tf_op jit(solution)/shard_map/ppermute | solution.py:102
  181.4 1.1 collective-permute-done.2
  182.6 18.3 %all_to_all.50 = f32[4,64,8,128]{3,2,1,0:T(8,128)S(1)} all-to-all(f32[4,64,8,128]{3,2,1,0:T(8,128)S(1)} %broadcast_in_dim.48), channel_id=1, replica_groups=mesh['x'=4,'z'=16,'core'=2,'rhs'=4] {'x'}, dimensions={0} | all-to-all | bytes 2097152 | tf_op jit(solution)/shard_map/all_to_all | solution.py:104
  201.0 3.7 %collective-permute-start.3 = (f32[64,8,128]{2,1,0:T(8,128)S(1)}, f32[64,8,128]{2,1,0:T(8,128)}, u32[]{:S(2)}, u32[]{:S(2)}) collective-permute-start(f32[64,8,128]{2,1,0:T(8,128)S(1)} %reduce_sum.57), channel_id=1, source_target_pairs={{0,4},{4,0},{1,5},{5,1},{2,6},{6,2},{3,7},{7,3},{8,12},{12,8},{9,1... | collective-permute-start | bytes 786440 | tf_op jit(solution)/shard_map/ppermute | solution.py:105
  204.9 1.7 convolution_subtract_fusion.4
  206.6 1.0 select_bitcast_fusion.7
  207.7 1.7 fusion.11
  210.0 2.1 collective-permute-start.4
  212.1 1.3 collective-permute-done.4
  213.5 1.0 broadcast_in_dim.49
  214.5 3.5 %all-to-all-start.5 = ((f32[4,64,8,128]{3,2,1,0:T(8,128)}), f32[4,64,8,128]{3,2,1,0:T(8,128)S(1)}, u32[]{:S(2)}, u32[]{:S(2)}) async-start(f32[4,64,8,128]{3,2,1,0:T(8,128)} %broadcast_in_dim.49), calls=%async_computation.5 | async-start | bytes 2097152 | tf_op jit(solution)/shard_map/all_to_all | solution.py:104
  218.0 3.0 %collective-permute-start.8 = (f32[1024,128]{1,0:T(8,128)S(1)}, f32[1024,128]{1,0:T(8,128)}, u32[]{:S(2)}, u32[]{:S(2)}) collective-permute-start(f32[1024,128]{1,0:T(8,128)S(1)} %bitcast.226), channel_id=1, source_target_pairs={{0,8},{8,0},{16,24},{24,16},{32,40},{40,32},{48,56},{56,48},{64,72... | collective-permute-start | bytes 1572872 | tf_op jit(solution)/shard_map/ppermute | solution.py:110
  221.7 11.4 %all-to-all-done.5 = f32[4,64,8,128]{3,2,1,0:T(8,128)S(1)} async-done(((f32[4,64,8,128]{3,2,1,0:T(8,128)}), f32[4,64,8,128]{3,2,1,0:T(8,128)S(1)}, u32[]{:S(2)}, u32[]{:S(2)}) %all-to-all-start.5) | async-done | bytes 1048608 | tf_op jit(solution)/shard_map/all_to_all | solution.py:104
  233.2 2.9 collective-permute-start.5
  236.0 1.7 convolution_subtract_fusion.2
  237.9 1.7 convolution_subtract_fusion.1
  239.7 1.7 fusion.10
  242.0 1.9 collective-permute-start.6
  244.0 2.1 fusion.5
  246.0 3.0 %collective-permute-start.9 = (f32[1024,128]{1,0:T(8,128)S(1)}, f32[1024,128]{1,0:T(8,128)S(1)}, u32[]{:S(2)}, u32[]{:S(2)}) collective-permute-start(f32[1024,128]{1,0:T(8,128)S(1)} %bitcast.232), channel_id=1, source_target_pairs={{0,8},{8,0},{16,24},{24,16},{32,40},{40,32},{48,56},{56,48},{64,72... | collective-permute-start | bytes 1572872 | tf_op jit(solution)/shard_map/ppermute | solution.py:110
  249.1 1.1 broadcast_in_dim.50
  250.2 3.5 %all-to-all-start.6 = ((f32[4,64,8,128]{3,2,1,0:T(8,128)}), f32[4,64,8,128]{3,2,1,0:T(8,128)S(1)}, u32[]{:S(2)}, u32[]{:S(2)}) async-start(f32[4,64,8,128]{3,2,1,0:T(8,128)} %broadcast_in_dim.50), calls=%async_computation.6 | async-start | bytes 2097152 | tf_op jit(solution)/shard_map/all_to_all | solution.py:104
  253.7 1.3 constant_dynamic-update-slice_fusion.15
  255.6 2.7 fusion.4
  258.3 2.6 collective-permute-done.9
  261.5 2.1 convolution_bitcast_fusion.2
  263.6 3.2 %collective-permute-start.10 = (f32[1024,128]{1,0:T(8,128)S(1)}, f32[1024,128]{1,0:T(8,128)S(1)}, u32[]{:S(2)}, u32[]{:S(2)}) collective-permute-start(f32[1024,128]{1,0:T(8,128)S(1)} %bitcast.236), channel_id=1, source_target_pairs={{0,8},{8,0},{16,24},{24,16},{32,40},{40,32},{48,56},{56,48},{64,72... | collective-permute-start | bytes 1572872 | tf_op jit(solution)/shard_map/ppermute | solution.py:110
  266.8 1.3 all-to-all-done.6
  268.1 3.8 %collective-permute-start.7 = (f32[64,8,128]{2,1,0:T(8,128)S(1)}, f32[64,8,128]{2,1,0:T(8,128)S(1)}, u32[]{:S(2)}, u32[]{:S(2)}) collective-permute-start(f32[64,8,128]{2,1,0:T(8,128)S(1)} %reduce_sum.59), channel_id=1, source_target_pairs={{0,4},{4,0},{1,5},{5,1},{2,6},{6,2},{3,7},{7,3},{8,12},{12,8},{9,1... | collective-permute-start | bytes 786440 | tf_op jit(solution)/shard_map/ppermute | solution.py:105
  272.0 2.1 fusion.3
  274.2 2.3 collective-permute-start.11
  276.5 1.2 collective-permute-done.10
  277.7 0.9 convolution_bitcast_fusion.1
  278.6 0.9 fusion.2
  279.5 10.6 %collective-permute-done.11 = f32[1024,128]{1,0:T(8,128)S(1)} collective-permute-done((f32[1024,128]{1,0:T(8,128)S(1)}, f32[1024,128]{1,0:T(8,128)S(1)}, u32[]{:S(2)}, u32[]{:S(2)}) %collective-permute-start.11) | collective-permute-done | bytes 524320 | tf_op jit(solution)/shard_map/ppermute | solution.py:110
  290.1 0.9 convolution_bitcast_fusion
  291.0 1.9 fusion.9
  (84 shorter events, 14.3 us)
Async XLA Ops:
  6.5 95.0 %all-gather.5.cloned.1.call-start = ((), (), s32[]{:S(2)}) async-start(), calls=%async_computation.7 | async-start | bytes 1114112 | tf_op jit(solution)/shard_map/all_gather | solution.py:82
  13.4 15.3 %copy-start.2 = (f32[8,8,1024]{2,1,0:T(8,128)}, f32[8,8,1024]{2,1,0:T(8,128)S(1)}, u32[]{:S(2)}) copy-start(f32[8,8,1024]{2,1,0:T(8,128)S(1)} %get-tuple-element.34) | copy-start | bytes 786436
  15.8 10.5 %all-to-all-start = ((f32[64,4,256]{2,0,1:T(8,128)}), f32[64,4,256]{2,0,1:T(8,128)S(1)}, u32[]{:S(2)}, u32[]{:S(2)}) async-start(f32[64,4,256]{2,0,1:T(8,128)} %bitcast.223), calls=%async_computation | async-start | bytes 524288 | tf_op jit(solution)/shard_map/all_to_all | solution.py:22
  28.7 65.4 %all-to-all-start.1 = ((f32[128,2,640]{2,1,0:T(2,128)}), f32[128,2,640]{2,1,0:T(2,128)S(1)}, u32[]{:S(2)}, u32[]{:S(2)}) async-start(f32[128,2,640]{2,1,0:T(2,128)} %copy.87), calls=%async_computation.1 | async-start | bytes 1310720 | tf_op jit(solution)/shard_map/all_to_all | solution.py:50
  49.7 118.8 %all-gather.7.cloned.1.call-start = ((), (), s32[]{:S(2)}) async-start(), calls=%async_computation.8 | async-start | bytes 4456448 | tf_op jit(solution)/shard_map/all_gather | solution.py:82
  97.4 17.7 %all-to-all-start.2 = ((f32[16,32,128]{2,1,0:T(8,128)}), f32[16,32,128]{2,1,0:T(8,128)S(1)}, u32[]{:S(2)}, u32[]{:S(2)}) async-start(f32[16,32,128]{2,1,0:T(8,128)} %bitcast.23), calls=%async_computation.2 | async-start | bytes 524288 | tf_op jit(solution)/shard_map/all_to_all | solution.py:89
  115.7 8.6 %collective-permute-start = (f32[64,8,128]{2,1,0:T(8,128)S(1)}, f32[64,8,128]{2,1,0:T(8,128)S(1)}, u32[]{:S(2)}, u32[]{:S(2)}) collective-permute-start(f32[64,8,128]{2,1,0:T(8,128)S(1)} %select_bitcast_fusion.11), channel_id=1, source_target_pairs={{0,4},{4,0},{1,5},{5,1},{2,6},{6,2},{3,7},{7,3},{8,12},{12,8},{9,1... | collective-permute-start | bytes 786440 | tf_op jit(solution)/shard_map/ppermute | solution.py:102
  124.4 22.8 %copy-start.1 = (f32[32,8,1024]{2,1,0:T(8,128)S(1)}, f32[32,8,1024]{2,1,0:T(8,128)}, u32[]{:S(2)}) copy-start(f32[32,8,1024]{2,1,0:T(8,128)} %all-gather.5.cloned.1.call-done) | copy-start | bytes 3145732
  142.2 4.8 %collective-permute-start.1 = (f32[64,8,128]{2,1,0:T(8,128)S(1)}, f32[64,8,128]{2,1,0:T(8,128)S(1)}, u32[]{:S(2)}, u32[]{:S(2)}) collective-permute-start(f32[64,8,128]{2,1,0:T(8,128)S(1)} %reduce_sum.56), channel_id=1, source_target_pairs={{0,4},{4,0},{1,5},{5,1},{2,6},{6,2},{3,7},{7,3},{8,12},{12,8},{9,1... | collective-permute-start | bytes 786440 | tf_op jit(solution)/shard_map/ppermute | solution.py:105
  170.8 11.7 %collective-permute-start.2 = (f32[64,8,128]{2,1,0:T(8,128)S(1)}, f32[64,8,128]{2,1,0:T(8,128)S(1)}, u32[]{:S(2)}, u32[]{:S(2)}) collective-permute-start(f32[64,8,128]{2,1,0:T(8,128)S(1)} %select_bitcast_fusion.8), channel_id=1, source_target_pairs={{0,4},{4,0},{1,5},{5,1},{2,6},{6,2},{3,7},{7,3},{8,12},{12,8},{9,1... | collective-permute-start | bytes 786440 | tf_op jit(solution)/shard_map/ppermute | solution.py:102
  201.0 5.6 %collective-permute-start.3 = (f32[64,8,128]{2,1,0:T(8,128)S(1)}, f32[64,8,128]{2,1,0:T(8,128)}, u32[]{:S(2)}, u32[]{:S(2)}) collective-permute-start(f32[64,8,128]{2,1,0:T(8,128)S(1)} %reduce_sum.57), channel_id=1, source_target_pairs={{0,4},{4,0},{1,5},{5,1},{2,6},{6,2},{3,7},{7,3},{8,12},{12,8},{9,1... | collective-permute-start | bytes 786440 | tf_op jit(solution)/shard_map/ppermute | solution.py:105
  210.0 3.4 %collective-permute-start.4 = (f32[64,8,128]{2,1,0:T(8,128)S(1)}, f32[64,8,128]{2,1,0:T(8,128)S(1)}, u32[]{:S(2)}, u32[]{:S(2)}) collective-permute-start(f32[64,8,128]{2,1,0:T(8,128)S(1)} %select_bitcast_fusion.5), channel_id=1, source_target_pairs={{0,4},{4,0},{1,5},{5,1},{2,6},{6,2},{3,7},{7,3},{8,12},{12,8},{9,1... | collective-permute-start | bytes 786440 | tf_op jit(solution)/shard_map/ppermute | solution.py:102
  214.5 18.6 %all-to-all-start.5 = ((f32[4,64,8,128]{3,2,1,0:T(8,128)}), f32[4,64,8,128]{3,2,1,0:T(8,128)S(1)}, u32[]{:S(2)}, u32[]{:S(2)}) async-start(f32[4,64,8,128]{3,2,1,0:T(8,128)} %broadcast_in_dim.49), calls=%async_computation.5 | async-start | bytes 2097152 | tf_op jit(solution)/shard_map/all_to_all | solution.py:104
  218.0 35.7 %collective-permute-start.8 = (f32[1024,128]{1,0:T(8,128)S(1)}, f32[1024,128]{1,0:T(8,128)}, u32[]{:S(2)}, u32[]{:S(2)}) collective-permute-start(f32[1024,128]{1,0:T(8,128)S(1)} %bitcast.226), channel_id=1, source_target_pairs={{0,8},{8,0},{16,24},{24,16},{32,40},{40,32},{48,56},{56,48},{64,72... | collective-permute-start | bytes 1572872 | tf_op jit(solution)/shard_map/ppermute | solution.py:110
  233.2 6.4 %collective-permute-start.5 = (f32[64,8,128]{2,1,0:T(8,128)S(1)}, f32[64,8,128]{2,1,0:T(8,128)S(1)}, u32[]{:S(2)}, u32[]{:S(2)}) collective-permute-start(f32[64,8,128]{2,1,0:T(8,128)S(1)} %reduce_sum.58), channel_id=1, source_target_pairs={{0,4},{4,0},{1,5},{5,1},{2,6},{6,2},{3,7},{7,3},{8,12},{12,8},{9,1... | collective-permute-start | bytes 786440 | tf_op jit(solution)/shard_map/ppermute | solution.py:105
  242.0 7.0 %collective-permute-start.6 = (f32[64,8,128]{2,1,0:T(8,128)S(1)}, f32[64,8,128]{2,1,0:T(8,128)S(1)}, u32[]{:S(2)}, u32[]{:S(2)}) collective-permute-start(f32[64,8,128]{2,1,0:T(8,128)S(1)} %select_bitcast_fusion.2), channel_id=1, source_target_pairs={{0,4},{4,0},{1,5},{5,1},{2,6},{6,2},{3,7},{7,3},{8,12},{12,8},{9,1... | collective-permute-start | bytes 786440 | tf_op jit(solution)/shard_map/ppermute | solution.py:102
  246.0 14.9 %collective-permute-start.9 = (f32[1024,128]{1,0:T(8,128)S(1)}, f32[1024,128]{1,0:T(8,128)S(1)}, u32[]{:S(2)}, u32[]{:S(2)}) collective-permute-start(f32[1024,128]{1,0:T(8,128)S(1)} %bitcast.232), channel_id=1, source_target_pairs={{0,8},{8,0},{16,24},{24,16},{32,40},{40,32},{48,56},{56,48},{64,72... | collective-permute-start | bytes 1572872 | tf_op jit(solution)/shard_map/ppermute | solution.py:110
  250.2 17.9 %all-to-all-start.6 = ((f32[4,64,8,128]{3,2,1,0:T(8,128)}), f32[4,64,8,128]{3,2,1,0:T(8,128)S(1)}, u32[]{:S(2)}, u32[]{:S(2)}) async-start(f32[4,64,8,128]{3,2,1,0:T(8,128)} %broadcast_in_dim.50), calls=%async_computation.6 | async-start | bytes 2097152 | tf_op jit(solution)/shard_map/all_to_all | solution.py:104
  258.3 15.8 %copy-start.3 = (f32[256,128]{1,0:T(8,128)S(1)}, f32[256,128]{1,0:T(8,128)}, u32[]{:S(2)}) copy-start(f32[256,128]{1,0:T(8,128)} %constant_dynamic-update-slice_fusion.10) | copy-start | bytes 393220
  263.6 15.0 %copy-start.4 = (f32[256,128]{1,0:T(8,128)S(1)}, f32[256,128]{1,0:T(8,128)}, u32[]{:S(2)}) copy-start(f32[256,128]{1,0:T(8,128)} %constant_dynamic-update-slice_fusion.14) | copy-start | bytes 393220
  263.6 14.1 %collective-permute-start.10 = (f32[1024,128]{1,0:T(8,128)S(1)}, f32[1024,128]{1,0:T(8,128)S(1)}, u32[]{:S(2)}, u32[]{:S(2)}) collective-permute-start(f32[1024,128]{1,0:T(8,128)S(1)} %bitcast.236), channel_id=1, source_target_pairs={{0,8},{8,0},{16,24},{24,16},{32,40},{40,32},{48,56},{56,48},{64,72... | collective-permute-start | bytes 1572872 | tf_op jit(solution)/shard_map/ppermute | solution.py:110
  268.1 9.6 %copy-start = (f32[256,4096]{1,0:T(8,128)S(1)}, f32[256,4096]{1,0:T(8,128)}, u32[]{:S(2)}) copy-start(f32[256,4096]{1,0:T(8,128)} %param.10) | copy-start | bytes 12582916
  268.1 6.0 %collective-permute-start.7 = (f32[64,8,128]{2,1,0:T(8,128)S(1)}, f32[64,8,128]{2,1,0:T(8,128)S(1)}, u32[]{:S(2)}, u32[]{:S(2)}) collective-permute-start(f32[64,8,128]{2,1,0:T(8,128)S(1)} %reduce_sum.59), channel_id=1, source_target_pairs={{0,4},{4,0},{1,5},{5,1},{2,6},{6,2},{3,7},{7,3},{8,12},{12,8},{9,1... | collective-permute-start | bytes 786440 | tf_op jit(solution)/shard_map/ppermute | solution.py:105
  274.2 15.9 %collective-permute-start.11 = (f32[1024,128]{1,0:T(8,128)S(1)}, f32[1024,128]{1,0:T(8,128)S(1)}, u32[]{:S(2)}, u32[]{:S(2)}) collective-permute-start(f32[1024,128]{1,0:T(8,128)S(1)} %bitcast.245), channel_id=1, source_target_pairs={{0,8},{8,0},{16,24},{24,16},{32,40},{40,32},{48,56},{56,48},{64,72... | collective-permute-start | bytes 1572872 | tf_op jit(solution)/shard_map/ppermute | solution.py:110
Sparse Core Ops, SparseCore 0:
  14.2 78.4 all-gather.4
  94.8 73.6 all-gather.6
where the time goes:
time: 303 us; the launch traced here: 301 us
  waiting for transfers between devices  112 us (37%)
  starting transfers between devices  84.8 us (28%)
  blocking collectives  36 us (12%)
  matrix products  27 us (9%)
  local copies, waits for them, and re-layouts  20.1 us (7%)
  between operations  14.1 us (5%)
  other arithmetic  6.71 us (2%)
    all_to_all x1, waiting for transfers between devices, redistribute(): lax.all_to_all(jnp.stack(halves, axis=1), ROWS, split_axis=0, concat_axis...  43.7 us
    all_to_all x2, blocking collectives, shards(): lax.all_to_all(copies, 'x', split_axis=0, concat_axis=0, tiled=True)  36 us
    dot_general x23, matrix products, product(): lax.dot_general(left, right, (contract, ((), ())), precision=lax.Precisio...  27 us
    ppermute x4, starting transfers between devices, shards(): half = keep + lax.ppermute(give, 'core', SWAP)  22.1 us
    all_to_all x1, starting transfers between devices, redistribute(): lax.all_to_all(jnp.stack(halves, axis=1), ROWS, split_axis=0, concat_axis...  21 us
    all_gather x2, waiting for transfers between devices, shards(): gathered = lax.all_gather(jnp.stack([tile(j, k) for j, k in names]), 'z')  20.7 us
    ppermute x4, waiting for transfers between devices, shards(): traded = lax.ppermute(solved, 'z', [(i, i ^ 1) for i in range(nz)])  14.4 us
    ppermute x4, starting transfers between devices, shards(): other = lax.ppermute(mine, 'core', SWAP)  14.1 us
  transfers between devices with their start and end apart: 19, of which 13 were waited for; matrix products, arithmetic and copies ran while one was open for 12% of the time, Pallas kernels for 0%

commit v1 on v0

--- a/solution.py
+++ b/solution.py
@@ -5,6 +5,18 @@
 
 ROWS = ("x", "z", "core")
 SWAP = [(0, 1), (1, 0)]
+
+
+def in_blocks(x, dim, size):
+    shape = x.shape
+    blocks = x.reshape(*shape[:dim], size, shape[dim] // size, *shape[dim + 1 :])
+    return jnp.moveaxis(blocks, dim, 0)
+
+
+def joined_along(blocks, dim):
+    dims = list(blocks.shape[1:])
+    dims[dim] *= blocks.shape[0]
+    return jnp.moveaxis(blocks, 0, dim).reshape(dims)
 
 
 def product(left, right, contract=((1,), (0,))):
@@ -19,7 +31,14 @@
 
 def redistribute(targets, send_order, send_count, recv_slot):
     groups = lax.axis_size(ROWS)
-    arrived = lax.all_to_all(targets, "rhs", split_axis=1, concat_axis=0, tiled=True)
+    peers, place = (lax.axis_size("rhs"), lax.axis_index("rhs"))
+    parts = in_blocks(targets, 1, peers)
+    gathered_2 = [parts[place]]
+    for step in range(1, peers):
+        sent = parts[place ^ step]
+        gathered_2.append(lax.ppermute(sent, "rhs", [(i_2, i_2 ^ step) for i_2 in range(peers)]))
+    parts = jnp.stack(gathered_2)[place ^ jnp.arange(peers)]
+    arrived = joined_along(parts, 0)
     rows_local, columns = arrived.shape
     capacity, tag = (4, 64)
     counts = send_count[0]

time: 303 us -> 303 us (level)
  starting transfers between devices: 84.8 us -> 88.9 us
    ppermute x0 -> x3, starting transfers between devices: none -> 9.88 us  [redistribute(): lax.ppermute(sent, 'rhs', [(i_2, i_2 ^ step) for i_2 in range(peers)])]
    all_to_all x1 -> x0, starting transfers between devices: 5.01 us -> none  [redistribute(): lax.all_to_all(targets, 'rhs', split_axis=1, concat_axis=0, tiled=True)]
    unnamed x27 -> x31, local copies, waits for them, and re-layouts: 8.48 us -> 8.51 us
  transfers between devices with their start and end apart: 19 -> 21, of which waited for: 13 -> 12; matrix products, arithmetic and copies ran while one was open for 12% -> 12% of each run, Pallas kernels for 0% -> 0%
where the time goes in v1:
time: 303 us; the launch traced here: 301 us
  waiting for transfers between devices  109 us (36%)
  starting transfers between devices  88.9 us (29%)
  blocking collectives  34.2 us (11%)
  matrix products  27 us (9%)
  local copies, waits for them, and re-layouts  20.3 us (7%)
  between operations  14.3 us (5%)
  other arithmetic  6.73 us (2%)
    all_to_all x1, waiting for transfers between devices, redistribute(): lax.all_to_all(jnp.stack(halves, axis=1), ROWS, split_axis=0, concat_axis...  44.1 us
    all_to_all x2, blocking collectives, shards(): lax.all_to_all(copies, 'x', split_axis=0, concat_axis=0, tiled=True)  34.2 us
    dot_general x23, matrix products, product(): lax.dot_general(left, right, (contract, ((), ())), precision=lax.Precisio...  27 us
    ppermute x4, starting transfers between devices, shards(): half = keep + lax.ppermute(give, 'core', SWAP)  21.8 us
    all_to_all x1, starting transfers between devices, redistribute(): lax.all_to_all(jnp.stack(halves, axis=1), ROWS, split_axis=0, concat_axis...  21.1 us
    all_gather x2, waiting for transfers between devices, shards(): gathered = lax.all_gather(jnp.stack([tile(j, k) for j, k in names]), 'z')  19.9 us
    ppermute x4, starting transfers between devices, shards(): other = lax.ppermute(mine, 'core', SWAP)  14.3 us
    ppermute x4, waiting for transfers between devices, shards(): traded = lax.ppermute(solved, 'z', [(i, i ^ 1) for i in range(nz)])  14.2 us
  transfers between devices with their start and end apart: 21, of which 12 were waited for; matrix products, arithmetic and copies ran while one was open for 12% of the time, Pallas kernels for 0%

profile of v1, /device:TPU:1, one launch (start us, length us, event | category | flops | bytes accessed | tf_op | source)
XLA Modules:
  0.0 300.6 jit_solution(14723104141056320887)
XLA Ops:
  6.5 0.8 slice_bitcast_fusion.29
  7.3 0.8 constant_dynamic-update-slice_fusion.7
  8.1 0.8 constant_dynamic-update-slice_fusion.6
  8.8 0.8 constant_dynamic-update-slice_fusion.5
  9.6 0.8 constant_dynamic-update-slice_fusion.4
  10.3 0.8 constant_dynamic-update-slice_fusion.3
  11.1 0.8 constant_dynamic-update-slice_fusion.2
  11.9 0.8 constant_dynamic-update-slice_fusion.1
  12.6 0.8 constant_dynamic-update-slice_fusion
  14.1 1.1 reshape.142
  15.4 5.5 %collective-permute-start.2 = (f32[64,256]{1,0:T(8,128)S(1)}, f32[64,256]{1,0:T(8,128)S(1)}, u32[]{:S(2)}, u32[]{:S(2)}) collective-permute-start(f32[64,256]{1,0:T(8,128)S(1)} %bitcast.276), channel_id=1, source_target_pairs={{0,3},{1,2},{2,1},{3,0},{4,7},{5,6},{6,5},{7,4},{8,11},{9,10},{10,... | collective-permute-start | bytes 196616 | tf_op jit(solution)/shard_map/ppermute | solution.py:39
  20.9 2.3 collective-permute-start.1
  23.2 2.1 collective-permute-start
  26.2 0.8 select_reduce_fusion
  29.9 1.4 copy.82
  31.3 21.1 %all-to-all-start = ((f32[128,2,640]{2,1,0:T(2,128)}), f32[128,2,640]{2,1,0:T(2,128)S(1)}, u32[]{:S(2)}, u32[]{:S(2)}) async-start(f32[128,2,640]{2,1,0:T(2,128)} %copy.82), calls=%async_computation | async-start | bytes 1310720 | tf_op jit(solution)/shard_map/all_to_all | solution.py:69
  53.2 44.1 %all-to-all-done = f32[128,2,640]{2,1,0:T(2,128)S(1)} async-done(((f32[128,2,640]{2,1,0:T(2,128)}), f32[128,2,640]{2,1,0:T(2,128)S(1)}, u32[]{:S(2)}, u32[]{:S(2)}) %all-to-all-start) | async-done | bytes 655392 | tf_op jit(solution)/shard_map/all_to_all | solution.py:69
  100.6 3.5 %all-to-all-start.1 = ((f32[16,32,128]{2,1,0:T(8,128)}), f32[16,32,128]{2,1,0:T(8,128)S(1)}, u32[]{:S(2)}, u32[]{:S(2)}) async-start(f32[16,32,128]{2,1,0:T(8,128)} %bitcast.26), calls=%async_computation.1 | async-start | bytes 524288 | tf_op jit(solution)/shard_map/all_to_all | solution.py:108
  104.2 1.1 slice_bitcast_fusion.15
  105.4 12.4 %all-to-all-done.1 = f32[16,32,128]{2,1,0:T(8,128)S(1)} async-done(((f32[16,32,128]{2,1,0:T(8,128)}), f32[16,32,128]{2,1,0:T(8,128)S(1)}, u32[]{:S(2)}, u32[]{:S(2)}) %all-to-all-start.1) | async-done | bytes 262176 | tf_op jit(solution)/shard_map/all_to_all | solution.py:108
  118.4 7.4 %collective-permute-start.3 = (f32[64,8,128]{2,1,0:T(8,128)S(1)}, f32[64,8,128]{2,1,0:T(8,128)S(1)}, u32[]{:S(2)}, u32[]{:S(2)}) collective-permute-start(f32[64,8,128]{2,1,0:T(8,128)S(1)} %select_bitcast_fusion.11), channel_id=1, source_target_pairs={{0,4},{4,0},{1,5},{5,1},{2,6},{6,2},{3,7},{7,3},{8,12},{12,8},{9,1... | collective-permute-start | bytes 786440 | tf_op jit(solution)/shard_map/ppermute | solution.py:121
  125.8 1.1 collective-permute-done.3
  127.1 17.0 %all_to_all.30 = f32[4,64,8,128]{3,2,1,0:T(8,128)S(1)} all-to-all(f32[4,64,8,128]{3,2,1,0:T(8,128)S(1)} %broadcast_in_dim.47), channel_id=1, replica_groups=mesh['x'=4,'z'=16,'core'=2,'rhs'=4] {'x'}, dimensions={0} | all-to-all | bytes 2097152 | tf_op jit(solution)/shard_map/all_to_all | solution.py:123
  144.2 3.7 %collective-permute-start.4 = (f32[64,8,128]{2,1,0:T(8,128)S(1)}, f32[64,8,128]{2,1,0:T(8,128)S(1)}, u32[]{:S(2)}, u32[]{:S(2)}) collective-permute-start(f32[64,8,128]{2,1,0:T(8,128)S(1)} %reduce_sum.56), channel_id=1, source_target_pairs={{0,4},{4,0},{1,5},{5,1},{2,6},{6,2},{3,7},{7,3},{8,12},{12,8},{9,1... | collective-permute-start | bytes 786440 | tf_op jit(solution)/shard_map/ppermute | solution.py:124
  147.9 1.1 collective-permute-done.4
  149.9 19.9 %all-gather.7.cloned.1.call-done = f32[128,8,1024]{2,1,0:T(8,128)} async-done(((f32[8,8,1024]{2,1,0:T(8,128)}), f32[128,8,1024]{2,1,0:T(8,128)}) %all-gather.7.cloned.1.call-update) | async-done | bytes 4194320 | tf_op jit(solution)/shard_map/all_gather | solution.py:101
  169.8 1.5 slice_bitcast_fusion.6
  172.0 10.5 %collective-permute-start.5 = (f32[64,8,128]{2,1,0:T(8,128)S(1)}, f32[64,8,128]{2,1,0:T(8,128)S(1)}, u32[]{:S(2)}, u32[]{:S(2)}) collective-permute-start(f32[64,8,128]{2,1,0:T(8,128)S(1)} %select_bitcast_fusion.8), channel_id=1, source_target_pairs={{0,4},{4,0},{1,5},{5,1},{2,6},{6,2},{3,7},{7,3},{8,12},{12,8},{9,1... | collective-permute-start | bytes 786440 | tf_op jit(solution)/shard_map/ppermute | solution.py:121
  182.6 1.1 collective-permute-done.5
  183.8 17.2 %all_to_all.31 = f32[4,64,8,128]{3,2,1,0:T(8,128)S(1)} all-to-all(f32[4,64,8,128]{3,2,1,0:T(8,128)S(1)} %broadcast_in_dim.48), channel_id=1, replica_groups=mesh['x'=4,'z'=16,'core'=2,'rhs'=4] {'x'}, dimensions={0} | all-to-all | bytes 2097152 | tf_op jit(solution)/shard_map/all_to_all | solution.py:123
  201.1 3.9 %collective-permute-start.6 = (f32[64,8,128]{2,1,0:T(8,128)S(1)}, f32[64,8,128]{2,1,0:T(8,128)}, u32[]{:S(2)}, u32[]{:S(2)}) collective-permute-start(f32[64,8,128]{2,1,0:T(8,128)S(1)} %reduce_sum.57), channel_id=1, source_target_pairs={{0,4},{4,0},{1,5},{5,1},{2,6},{6,2},{3,7},{7,3},{8,12},{12,8},{9,1... | collective-permute-start | bytes 786440 | tf_op jit(solution)/shard_map/ppermute | solution.py:124
  205.2 1.7 convolution_subtract_fusion.4
  206.9 1.0 select_bitcast_fusion.7
  207.9 1.7 fusion.11
  210.2 1.9 collective-permute-start.7
  212.2 1.5 collective-permute-done.7
  213.7 1.0 broadcast_in_dim.49
  214.7 3.5 %all-to-all-start.4 = ((f32[4,64,8,128]{3,2,1,0:T(8,128)}), f32[4,64,8,128]{3,2,1,0:T(8,128)S(1)}, u32[]{:S(2)}, u32[]{:S(2)}) async-start(f32[4,64,8,128]{3,2,1,0:T(8,128)} %broadcast_in_dim.49), calls=%async_computation.4 | async-start | bytes 2097152 | tf_op jit(solution)/shard_map/all_to_all | solution.py:123
  218.3 2.8 collective-permute-start.11
  221.7 11.7 %all-to-all-done.4 = f32[4,64,8,128]{3,2,1,0:T(8,128)S(1)} async-done(((f32[4,64,8,128]{3,2,1,0:T(8,128)}), f32[4,64,8,128]{3,2,1,0:T(8,128)S(1)}, u32[]{:S(2)}, u32[]{:S(2)}) %all-to-all-start.4) | async-done | bytes 1048608 | tf_op jit(solution)/shard_map/all_to_all | solution.py:123
  233.4 2.9 collective-permute-start.8
  236.3 1.7 convolution_subtract_fusion.2
  238.2 1.7 convolution_subtract_fusion.1
  240.0 1.7 fusion.10
  242.3 1.9 collective-permute-start.9
  244.2 2.1 fusion.5
  246.3 2.8 collective-permute-start.12
  249.1 1.0 broadcast_in_dim.50
  250.2 3.5 %all-to-all-start.5 = ((f32[4,64,8,128]{3,2,1,0:T(8,128)}), f32[4,64,8,128]{3,2,1,0:T(8,128)S(1)}, u32[]{:S(2)}, u32[]{:S(2)}) async-start(f32[4,64,8,128]{3,2,1,0:T(8,128)} %broadcast_in_dim.50), calls=%async_computation.5 | async-start | bytes 2097152 | tf_op jit(solution)/shard_map/all_to_all | solution.py:123
  253.7 1.3 constant_dynamic-update-slice_fusion.15
  255.6 2.7 fusion.4
  258.3 2.9 collective-permute-done.12
  261.7 2.1 convolution_bitcast_fusion.2
  263.8 2.9 collective-permute-start.13
  266.7 1.3 all-to-all-done.5
  268.1 3.8 %collective-permute-start.10 = (f32[64,8,128]{2,1,0:T(8,128)S(1)}, f32[64,8,128]{2,1,0:T(8,128)S(1)}, u32[]{:S(2)}, u32[]{:S(2)}) collective-permute-start(f32[64,8,128]{2,1,0:T(8,128)S(1)} %reduce_sum.59), channel_id=1, source_target_pairs={{0,4},{4,0},{1,5},{5,1},{2,6},{6,2},{3,7},{7,3},{8,12},{12,8},{9,1... | collective-permute-start | bytes 786440 | tf_op jit(solution)/shard_map/ppermute | solution.py:124
  272.0 2.1 fusion.3
  274.2 2.7 collective-permute-start.14
  276.9 1.0 collective-permute-done.13
  277.9 0.9 convolution_bitcast_fusion.1
  278.9 0.9 fusion.2
  279.8 10.4 %collective-permute-done.14 = f32[1024,128]{1,0:T(8,128)S(1)} collective-permute-done((f32[1024,128]{1,0:T(8,128)S(1)}, f32[1024,128]{1,0:T(8,128)S(1)}, u32[]{:S(2)}, u32[]{:S(2)}) %collective-permute-start.14) | collective-permute-done | bytes 524320 | tf_op jit(solution)/shard_map/ppermute | solution.py:129
  290.1 0.9 convolution_bitcast_fusion
  291.0 1.9 fusion.9
  (97 shorter events, 15.9 us)
Async XLA Ops:
  6.5 97.6 %all-gather.5.cloned.1.call-start = ((), (), s32[]{:S(2)}) async-start(), calls=%async_computation.6 | async-start | bytes 1114112 | tf_op jit(solution)/shard_map/all_gather | solution.py:101
  13.4 16.5 %copy-start.2 = (f32[8,8,1024]{2,1,0:T(8,128)}, f32[8,8,1024]{2,1,0:T(8,128)S(1)}, u32[]{:S(2)}) copy-start(f32[8,8,1024]{2,1,0:T(8,128)S(1)} %get-tuple-element.38) | copy-start | bytes 786436
  15.4 12.9 %collective-permute-start.2 = (f32[64,256]{1,0:T(8,128)S(1)}, f32[64,256]{1,0:T(8,128)S(1)}, u32[]{:S(2)}, u32[]{:S(2)}) collective-permute-start(f32[64,256]{1,0:T(8,128)S(1)} %bitcast.276), channel_id=1, source_target_pairs={{0,3},{1,2},{2,1},{3,0},{4,7},{5,6},{6,5},{7,4},{8,11},{9,10},{10,... | collective-permute-start | bytes 196616 | tf_op jit(solution)/shard_map/ppermute | solution.py:39
  20.9 7.4 %collective-permute-start.1 = (f32[64,256]{1,0:T(8,128)S(1)}, f32[64,256]{1,0:T(8,128)S(1)}, u32[]{:S(2)}, u32[]{:S(2)}) collective-permute-start(f32[64,256]{1,0:T(8,128)S(1)} %bitcast.277), channel_id=1, source_target_pairs={{0,2},{1,3},{2,0},{3,1},{4,6},{5,7},{6,4},{7,5},{8,10},{9,11},{10,... | collective-permute-start | bytes 196616 | tf_op jit(solution)/shard_map/ppermute | solution.py:39
  23.2 5.1 %collective-permute-start = (f32[64,256]{1,0:T(8,128)S(1)}, f32[64,256]{1,0:T(8,128)S(1)}, u32[]{:S(2)}, u32[]{:S(2)}) collective-permute-start(f32[64,256]{1,0:T(8,128)S(1)} %bitcast.278), channel_id=1, source_target_pairs={{0,1},{1,0},{2,3},{3,2},{4,5},{5,4},{6,7},{7,6},{8,9},{9,8},{10,11... | collective-permute-start | bytes 196616 | tf_op jit(solution)/shard_map/ppermute | solution.py:39
  31.3 66.0 %all-to-all-start = ((f32[128,2,640]{2,1,0:T(2,128)}), f32[128,2,640]{2,1,0:T(2,128)S(1)}, u32[]{:S(2)}, u32[]{:S(2)}) async-start(f32[128,2,640]{2,1,0:T(2,128)} %copy.82), calls=%async_computation | async-start | bytes 1310720 | tf_op jit(solution)/shard_map/all_to_all | solution.py:69
  52.4 117.3 %all-gather.7.cloned.1.call-start = ((), (), s32[]{:S(2)}) async-start(), calls=%async_computation.7 | async-start | bytes 4456448 | tf_op jit(solution)/shard_map/all_gather | solution.py:101
  100.6 17.2 %all-to-all-start.1 = ((f32[16,32,128]{2,1,0:T(8,128)}), f32[16,32,128]{2,1,0:T(8,128)S(1)}, u32[]{:S(2)}, u32[]{:S(2)}) async-start(f32[16,32,128]{2,1,0:T(8,128)} %bitcast.26), calls=%async_computation.1 | async-start | bytes 524288 | tf_op jit(solution)/shard_map/all_to_all | solution.py:108
  118.4 8.6 %collective-permute-start.3 = (f32[64,8,128]{2,1,0:T(8,128)S(1)}, f32[64,8,128]{2,1,0:T(8,128)S(1)}, u32[]{:S(2)}, u32[]{:S(2)}) collective-permute-start(f32[64,8,128]{2,1,0:T(8,128)S(1)} %select_bitcast_fusion.11), channel_id=1, source_target_pairs={{0,4},{4,0},{1,5},{5,1},{2,6},{6,2},{3,7},{7,3},{8,12},{12,8},{9,1... | collective-permute-start | bytes 786440 | tf_op jit(solution)/shard_map/ppermute | solution.py:121
  127.0 22.2 %copy-start.1 = (f32[32,8,1024]{2,1,0:T(8,128)S(1)}, f32[32,8,1024]{2,1,0:T(8,128)}, u32[]{:S(2)}) copy-start(f32[32,8,1024]{2,1,0:T(8,128)} %all-gather.5.cloned.1.call-done) | copy-start | bytes 3145732
  144.2 4.8 %collective-permute-start.4 = (f32[64,8,128]{2,1,0:T(8,128)S(1)}, f32[64,8,128]{2,1,0:T(8,128)S(1)}, u32[]{:S(2)}, u32[]{:S(2)}) collective-permute-start(f32[64,8,128]{2,1,0:T(8,128)S(1)} %reduce_sum.56), channel_id=1, source_target_pairs={{0,4},{4,0},{1,5},{5,1},{2,6},{6,2},{3,7},{7,3},{8,12},{12,8},{9,1... | collective-permute-start | bytes 786440 | tf_op jit(solution)/shard_map/ppermute | solution.py:124
  172.0 11.7 %collective-permute-start.5 = (f32[64,8,128]{2,1,0:T(8,128)S(1)}, f32[64,8,128]{2,1,0:T(8,128)S(1)}, u32[]{:S(2)}, u32[]{:S(2)}) collective-permute-start(f32[64,8,128]{2,1,0:T(8,128)S(1)} %select_bitcast_fusion.8), channel_id=1, source_target_pairs={{0,4},{4,0},{1,5},{5,1},{2,6},{6,2},{3,7},{7,3},{8,12},{12,8},{9,1... | collective-permute-start | bytes 786440 | tf_op jit(solution)/shard_map/ppermute | solution.py:121
  201.1 5.8 %collective-permute-start.6 = (f32[64,8,128]{2,1,0:T(8,128)S(1)}, f32[64,8,128]{2,1,0:T(8,128)}, u32[]{:S(2)}, u32[]{:S(2)}) collective-permute-start(f32[64,8,128]{2,1,0:T(8,128)S(1)} %reduce_sum.57), channel_id=1, source_target_pairs={{0,4},{4,0},{1,5},{5,1},{2,6},{6,2},{3,7},{7,3},{8,12},{12,8},{9,1... | collective-permute-start | bytes 786440 | tf_op jit(solution)/shard_map/ppermute | solution.py:124
  210.2 3.4 %collective-permute-start.7 = (f32[64,8,128]{2,1,0:T(8,128)S(1)}, f32[64,8,128]{2,1,0:T(8,128)S(1)}, u32[]{:S(2)}, u32[]{:S(2)}) collective-permute-start(f32[64,8,128]{2,1,0:T(8,128)S(1)} %select_bitcast_fusion.5), channel_id=1, source_target_pairs={{0,4},{4,0},{1,5},{5,1},{2,6},{6,2},{3,7},{7,3},{8,12},{12,8},{9,1... | collective-permute-start | bytes 786440 | tf_op jit(solution)/shard_map/ppermute | solution.py:121
  214.7 18.6 %all-to-all-start.4 = ((f32[4,64,8,128]{3,2,1,0:T(8,128)}), f32[4,64,8,128]{3,2,1,0:T(8,128)S(1)}, u32[]{:S(2)}, u32[]{:S(2)}) async-start(f32[4,64,8,128]{3,2,1,0:T(8,128)} %broadcast_in_dim.49), calls=%async_computation.4 | async-start | bytes 2097152 | tf_op jit(solution)/shard_map/all_to_all | solution.py:123
  218.3 35.4 %collective-permute-start.11 = (f32[1024,128]{1,0:T(8,128)S(1)}, f32[1024,128]{1,0:T(8,128)}, u32[]{:S(2)}, u32[]{:S(2)}) collective-permute-start(f32[1024,128]{1,0:T(8,128)S(1)} %bitcast.237), channel_id=1, source_target_pairs={{0,8},{8,0},{16,24},{24,16},{32,40},{40,32},{48,56},{56,48},{64,72... | collective-permute-start | bytes 1572872 | tf_op jit(solution)/shard_map/ppermute | solution.py:129
  233.4 6.4 %collective-permute-start.8 = (f32[64,8,128]{2,1,0:T(8,128)S(1)}, f32[64,8,128]{2,1,0:T(8,128)S(1)}, u32[]{:S(2)}, u32[]{:S(2)}) collective-permute-start(f32[64,8,128]{2,1,0:T(8,128)S(1)} %reduce_sum.58), channel_id=1, source_target_pairs={{0,4},{4,0},{1,5},{5,1},{2,6},{6,2},{3,7},{7,3},{8,12},{12,8},{9,1... | collective-permute-start | bytes 786440 | tf_op jit(solution)/shard_map/ppermute | solution.py:124
  242.3 6.8 %collective-permute-start.9 = (f32[64,8,128]{2,1,0:T(8,128)S(1)}, f32[64,8,128]{2,1,0:T(8,128)S(1)}, u32[]{:S(2)}, u32[]{:S(2)}) collective-permute-start(f32[64,8,128]{2,1,0:T(8,128)S(1)} %select_bitcast_fusion.2), channel_id=1, source_target_pairs={{0,4},{4,0},{1,5},{5,1},{2,6},{6,2},{3,7},{7,3},{8,12},{12,8},{9,1... | collective-permute-start | bytes 786440 | tf_op jit(solution)/shard_map/ppermute | solution.py:121
  246.3 14.9 %collective-permute-start.12 = (f32[1024,128]{1,0:T(8,128)S(1)}, f32[1024,128]{1,0:T(8,128)S(1)}, u32[]{:S(2)}, u32[]{:S(2)}) collective-permute-start(f32[1024,128]{1,0:T(8,128)S(1)} %bitcast.243), channel_id=1, source_target_pairs={{0,8},{8,0},{16,24},{24,16},{32,40},{40,32},{48,56},{56,48},{64,72... | collective-permute-start | bytes 1572872 | tf_op jit(solution)/shard_map/ppermute | solution.py:129
  250.2 17.9 %all-to-all-start.5 = ((f32[4,64,8,128]{3,2,1,0:T(8,128)}), f32[4,64,8,128]{3,2,1,0:T(8,128)S(1)}, u32[]{:S(2)}, u32[]{:S(2)}) async-start(f32[4,64,8,128]{3,2,1,0:T(8,128)} %broadcast_in_dim.50), calls=%async_computation.5 | async-start | bytes 2097152 | tf_op jit(solution)/shard_map/all_to_all | solution.py:123
  258.3 15.8 %copy-start.3 = (f32[256,128]{1,0:T(8,128)S(1)}, f32[256,128]{1,0:T(8,128)}, u32[]{:S(2)}) copy-start(f32[256,128]{1,0:T(8,128)} %constant_dynamic-update-slice_fusion.10) | copy-start | bytes 393220
  263.8 15.0 %copy-start.4 = (f32[256,128]{1,0:T(8,128)S(1)}, f32[256,128]{1,0:T(8,128)}, u32[]{:S(2)}) copy-start(f32[256,128]{1,0:T(8,128)} %constant_dynamic-update-slice_fusion.14) | copy-start | bytes 393220
  263.8 14.1 %collective-permute-start.13 = (f32[1024,128]{1,0:T(8,128)S(1)}, f32[1024,128]{1,0:T(8,128)S(1)}, u32[]{:S(2)}, u32[]{:S(2)}) collective-permute-start(f32[1024,128]{1,0:T(8,128)S(1)} %bitcast.247), channel_id=1, source_target_pairs={{0,8},{8,0},{16,24},{24,16},{32,40},{40,32},{48,56},{56,48},{64,72... | collective-permute-start | bytes 1572872 | tf_op jit(solution)/shard_map/ppermute | solution.py:129
  268.1 9.8 %copy-start = (f32[256,4096]{1,0:T(8,128)S(1)}, f32[256,4096]{1,0:T(8,128)}, u32[]{:S(2)}) copy-start(f32[256,4096]{1,0:T(8,128)} %param.10) | copy-start | bytes 12582916
  268.1 5.9 %collective-permute-start.10 = (f32[64,8,128]{2,1,0:T(8,128)S(1)}, f32[64,8,128]{2,1,0:T(8,128)S(1)}, u32[]{:S(2)}, u32[]{:S(2)}) collective-permute-start(f32[64,8,128]{2,1,0:T(8,128)S(1)} %reduce_sum.59), channel_id=1, source_target_pairs={{0,4},{4,0},{1,5},{5,1},{2,6},{6,2},{3,7},{7,3},{8,12},{12,8},{9,1... | collective-permute-start | bytes 786440 | tf_op jit(solution)/shard_map/ppermute | solution.py:124
  274.2 15.9 %collective-permute-start.14 = (f32[1024,128]{1,0:T(8,128)S(1)}, f32[1024,128]{1,0:T(8,128)S(1)}, u32[]{:S(2)}, u32[]{:S(2)}) collective-permute-start(f32[1024,128]{1,0:T(8,128)S(1)} %bitcast.256), channel_id=1, source_target_pairs={{0,8},{8,0},{16,24},{24,16},{32,40},{40,32},{48,56},{56,48},{64,72... | collective-permute-start | bytes 1572872 | tf_op jit(solution)/shard_map/ppermute | solution.py:129
Sparse Core Ops, SparseCore 0:
  14.2 78.9 all-gather.4
  95.2 74.4 all-gather.6
